TPU v7x, 32 devices: a whole 2x2x4 slice. The times are simulated.
32 devices in a mesh: seq: 4 (over y, x), tp: 8 (over z, core).
Axes of the slice: x: 2, y: 2, z: 4, core: 2. Of those that a mesh axis runs over, the one named last changes fastest.
Arguments:
- hidden: bfloat16 [4096, 4096], P(('seq', 'tp')), may hold values from -6 to 6
- norm_gain: float32 [4096], replicated, may hold values from 0.5 to 1.5
- inner_weight: bfloat16 [4096, 2, 2048], P(None, None, 'tp'), may hold values from -0.09375 to 0.09375
- group_weight: bfloat16 [4096, 1024], P(None, 'tp'), may hold values from -0.09375 to 0.09375
- step_weight: bfloat16 [4096, 32], P(None, 'tp'), may hold values from -0.09375 to 0.09375
- step_bias: float32 [32], P('tp'), may hold values from -2 to 1
- decay_rate: float32 [32], P('tp'), may hold values from 0.0001 to 0.1
- filter_inner: bfloat16 [4, 2048], P(None, 'tp'), may hold values from -3 to 3
- filter_group: bfloat16 [4, 1024], P(None, 'tp'), may hold values from -3 to 3
- skip_gain: float32 [32], P('tp'), may hold values from 0.5 to 1.5
- mixer_gain: float32 [2048], P('tp'), may hold values from 0.5 to 1.5
- output_weight: bfloat16 [2048, 4096], P('tp'), may hold values from -0.125 to 0.125
- segment_ids: int32 [4096], replicated, may hold values from 0 to 3, never falling along the last dimension, each value on 1 to 2048 neighbouring positions
Outputs:
- layer_out: bfloat16 [4096, 4096], P(('seq', 'tp'))
Inputs may be any that keep to these rules, and one draw needn't show every extreme that they name: `segment_ids`: ids never fall along the pack; every id names at least one token, and one request has exactly 2048 tokens.
All inputs are finite; a program needn't handle non-finite values.
Results may differ from a plain program's by a relative error of at most 0.0051.
Values may be sent and summed in bfloat16 or wider, within the bound.
A program may use at most 128 MiB of HBM per device.

v0:
```python
import jax
import jax.numpy as jnp
from jax import lax
from jax.sharding import PartitionSpec as P

STRETCH = 256
EPS = 1e-05
HIGH = lax.Precision.HIGHEST


def swapped(block, axis, stride):
    count = lax.axis_size(axis)
    route = []
    for low in range(count):
        high = low | 1 << stride
        if high != low and high < count:
            route += [(low, high), (high, low)]
    return lax.ppermute(block, axis, route)


def from_behind(array, axis, by):
    size = lax.axis_size(axis)
    pairs = [(i, i + by) for i in range(size) if 0 <= i + by < size]
    return lax.ppermute(array, axis, pairs)


def entering_2(value, axis, join, neutral):
    count, mine = (lax.axis_size(axis), lax.axis_index(axis))
    pieces = jax.tree.map(lambda part: lax.all_gather(part, axis), value)
    total = jax.tree.map(
        lambda part, zero: jnp.full_like(part, 0) + jnp.asarray(zero, part.dtype), value, neutral
    )

    def hop(position, total):
        longer = join(total, jax.tree.map(lambda part: part[position], pieces))
        return jax.tree.map(lambda new, old: jnp.where(position < mine, new, old), longer, total)

    return lax.fori_loop(0, count - 1, hop, total)


def combine(earlier, later):
    return (earlier[0] * later[0], later[0][:, None, None] * earlier[1] + later[1])


def body(
    hidden,
    norm_gain,
    inner_weight,
    group_weight,
    step_weight,
    step_bias,
    decay_rate,
    filter_inner,
    filter_group,
    skip_gain,
    mixer_gain,
    output_weight,
    segment_ids,
):
    rows = hidden.shape[0]
    length = rows * lax.axis_size("tp")
    width = hidden.shape[1]
    inner_dev = inner_weight.shape[2]
    heads_dev = step_weight.shape[1]
    head_dim = inner_dev // heads_dev
    state_dim = group_weight.shape[1]
    taps = filter_inner.shape[0]
    first_row = lax.axis_index("seq") * length
    is_first = lax.axis_index("tp") % 2 == 0
    hidden_f = hidden.astype(jnp.float32)
    normed = (
        hidden_f
        * lax.rsqrt(jnp.mean(hidden_f * hidden_f, axis=-1, keepdims=True) + EPS)
        * norm_gain
    ).astype(jnp.bfloat16)
    other_weight, other_filter = swapped((group_weight, filter_group), "tp", 0)
    group_cols = (
        jnp.where(is_first, group_weight, other_weight),
        jnp.where(is_first, other_weight, group_weight),
    )
    filters = jnp.concatenate(
        [
            filter_inner,
            jnp.where(is_first, filter_group, other_filter),
            jnp.where(is_first, other_filter, filter_group),
        ],
        axis=1,
    )
    matrices = (inner_weight.reshape(width, 2 * inner_dev),) + group_cols + (step_weight,)
    piece = lax.all_gather(normed, "tp", axis=0, tiled=True)
    projected = jnp.concatenate(
        [jnp.dot(piece, matrix, preferred_element_type=jnp.float32) for matrix in matrices], axis=1
    )
    gate_z = projected[:, :inner_dev]
    conv_in = projected[:, inner_dev:-heads_dev]
    step_raw = projected[:, -heads_dev:]
    seg_pad = jnp.concatenate([jnp.full((taps - 1,), -1, jnp.int32), segment_ids])
    seg_ext = lax.dynamic_slice_in_dim(seg_pad, first_row, length + taps - 1)
    seg_local = seg_ext[taps - 1 :]
    before = from_behind(conv_in[length - (taps - 1) :], "seq", 1)
    extended = jnp.concatenate([before, conv_in], axis=0)
    filters_f = filters.astype(jnp.float32)
    total = jnp.zeros_like(conv_in)
    for offset in range(taps):
        same = (seg_ext[offset : offset + length] == seg_local).astype(jnp.float32)
        total = total + filters_f[offset] * extended[offset : offset + length] * same[:, None]
    active = jax.nn.silu(total)
    inner_x = active[:, :inner_dev]
    input_map = active[:, inner_dev : inner_dev + state_dim]
    output_map = active[:, inner_dev + state_dim :]
    starts = seg_local != seg_ext[taps - 2 : taps - 2 + length]
    step = jax.nn.softplus(step_raw + step_bias)
    log_decay = -step * decay_rate
    blocks = length // STRETCH
    block_x = inner_x.reshape(blocks, STRETCH, heads_dev, head_dim)
    block_b = input_map.reshape(blocks, STRETCH, state_dim)
    block_c = output_map.reshape(blocks, STRETCH, state_dim)
    step_heads = step.reshape(blocks, STRETCH, heads_dev).transpose(0, 2, 1)
    cumul = jnp.cumsum(log_decay.reshape(blocks, STRETCH, heads_dev), axis=1).transpose(0, 2, 1)
    block_seg = seg_local.reshape(blocks, STRETCH)
    block_start = starts.reshape(blocks, STRETCH)
    causal = jnp.tril(jnp.ones((STRETCH, STRETCH), jnp.bool_))
    same_seg = ((block_seg[:, :, None] == block_seg[:, None, :]) & causal)[:, None]
    gaps = cumul[:, :, :, None] - cumul[:, :, None, :]
    decay = jnp.where(same_seg, jnp.exp(jnp.where(same_seg, gaps, 0.0)), 0.0)
    products = jnp.einsum("cin,cjn->cij", block_c, block_b, precision=HIGH)
    mixing = decay * products[:, None] * step_heads[:, :, None, :]
    local_y = jnp.einsum("chij,cjhp->cihp", mixing, block_x, precision=HIGH)
    same_last = (block_seg == block_seg[:, -1:])[:, None, :]
    last_gap = cumul[:, :, -1:] - cumul
    end_weight = (
        jnp.where(same_last, jnp.exp(jnp.where(same_last, last_gap, 0.0)), 0.0) * step_heads
    )
    block_state = jnp.einsum("chj,cjhp,cjn->chpn", end_weight, block_x, block_b, precision=HIGH)
    clean = jnp.logical_not(jnp.any(block_start, axis=1)).astype(jnp.float32)
    block_keep = jnp.exp(cumul[:, :, -1]) * clean[:, None]

    def carry_blocks(carry, inputs):
        acc_state, acc_keep = carry
        keep, fresh = inputs
        return ((keep[:, None, None] * acc_state + fresh, acc_keep * keep), (acc_state, acc_keep))

    empty_state = jnp.zeros((heads_dev, head_dim, state_dim), jnp.float32)
    unit_keep = jnp.ones((heads_dev,), jnp.float32)
    (device_state, device_keep), (prior_state, prior_keep) = lax.scan(
        carry_blocks, (empty_state, unit_keep), (block_keep, block_state)
    )
    entering = entering_2((device_keep, device_state), "seq", combine, (unit_keep, empty_state))
    incoming = entering[1]
    entry_state = prior_state + prior_keep[:, :, None, None] * incoming[None]
    alive = (jnp.cumsum(block_start.astype(jnp.int32), axis=1) == 0).astype(jnp.float32)
    entry_weight = jnp.exp(cumul) * alive[:, None, :]
    carried_y = jnp.einsum("chi,cin,chpn->cihp", entry_weight, block_c, entry_state, precision=HIGH)
    ssm_out = (local_y + carried_y).reshape(length, heads_dev, head_dim) + skip_gain[
        None, :, None
    ] * inner_x.reshape(length, heads_dev, head_dim)
    gated = ssm_out.reshape(length, inner_dev) * jax.nn.silu(gate_z)
    own_squares = jnp.sum(gated * gated, axis=-1)
    other_squares = swapped(own_squares, "tp", 0)
    group_mean = (own_squares + other_squares) / (2 * inner_dev)
    mixed = (gated * lax.rsqrt(group_mean + EPS)[:, None] * mixer_gain).astype(jnp.bfloat16)
    partial_out = jnp.dot(mixed, output_weight, preferred_element_type=jnp.float32)
    mine = lax.psum_scatter(partial_out, "tp", scatter_dimension=0, tiled=True)
    return (hidden_f + mine).astype(jnp.bfloat16)


def solution(mesh):
    in_specs = (
        P(("seq", "tp"), None),
        P(),
        P(None, None, "tp"),
        P(None, "tp"),
        P(None, "tp"),
        P("tp"),
        P("tp"),
        P(None, "tp"),
        P(None, "tp"),
        P("tp"),
        P("tp"),
        P("tp", None),
        P(),
    )
    out_specs = P(("seq", "tp"), None)
    return jax.shard_map(body, mesh=mesh, in_specs=in_specs, out_specs=out_specs, check_vma=False)
```

profile of v0, /device:TPU:0, one launch (start us, length us, event | category | flops | bytes accessed | tf_op | source)
XLA Modules:
  0.0 372.5 jit_solution(9451892559120451516)
XLA Ops:
  6.6 1.7 fusion.20
  8.3 2.5 fusion.22
  11.6 1.2 reduce-window.16
  14.8 4.9 %copy.92 = bf16[512,8,2,256]{3,1,2,0:T(8,128)(2,1)} copy(bf16[512,8,2,256]{3,2,1,0:T(2,128)(2,1)} %bitcast.91) | data formatting | bytes 8388608
  21.1 74.7 %all-gather.4.cloned.1.call-done = bf16[1024,4096]{1,0:T(8,128)(2,1)} async-done(((bf16[128,4096]{1,0:T(8,128)(2,1)}), bf16[1024,4096]{1,0:T(8,128)(2,1)}) %all-gather.4.cloned.1.call-update) | async-done | bytes 8388624 | tf_op jit(solution)/shard_map/all_gather | solution.py:90
  95.8 5.7 %negate_multiply_fusion = (f32[1024,4]{0,1:T(4,128)S(1)}, f32[1024,4]{0,1:T(4,128)S(1)}) fusion(f32[4]{0:T(128)S(1)} %copy-done.15, f32[4]{0:T(128)S(1)} %copy-done.16, bf16[1024,4096]{1,0:T(8,128)(2,1)} %all-gather.4.cloned.1.call-done, bf16[4096,4]{0,1:T(4,128)(2,1)S(1)} %copy-done.13), kind=kOutput, calls=%fused_computation.96 | convolution fusion | flops 33591296 | bytes 8454176 | tf_op jit(solution)/shard_map/dot_general | solution.py:92
  101.5 4.8 %reduce-window.14 = f32[4,4,2,128]{3,2,1,0:T(2,128)S(1)} reduce-window(f32[4,4,2,128]{3,2,1,0:T(2,128)S(1)} %copy.83, f32[]{:T(128)} %constant.89.clone.1), window={size=1x1x1x128 pad=0_0x0_0x0_0x127_0}, to_apply=%region_1.2 | reduce-window | flops 520192 | bytes 32772 | tf_op jit(solution)/shard_map/reduce-window
  107.2 6.7 %fusion.38 = f32[1024,128]{0,1:T(8,128)S(1)} fusion(bf16[1024,4096]{1,0:T(8,128)(2,1)} %all-gather.4.cloned.1.call-done, bf16[4096,128]{1,0:T(8,128)(2,1)} %collective-permute-done.1, bf16[4096,128]{1,0:T(8,128)(2,1)S(1)} %copy-done.7, pred[]{:T(512)S(6)} %eq.59), kind=kOutput, calls=%fused_computation.58 | convolution fusion | flops 1074266112 | bytes 11010049 | tf_op jit(solution)/shard_map/dot_general | solution.py:92
  113.8 2.9 fusion.40
  116.8 6.5 %fusion.78 = f32[1024,512]{0,1:T(8,128)S(1)} fusion(bf16[1024,4096]{1,0:T(8,128)(2,1)S(1)} %copy-done.1, bf16[4096,512]{1,0:T(8,128)(2,1)} %bitcast.92), kind=kOutput, calls=%fused_computation.123 | convolution fusion | flops 4294967296 | bytes 14680064 | tf_op jit(solution)/shard_map/dot_general | solution.py:92
  123.4 3.6 collective-permute-start.2
  127.4 5.9 %collective-permute-done.2 = f32[3,512]{0,1:T(8,128)S(1)} collective-permute-done((f32[3,512]{0,1:T(8,128)S(1)}, f32[3,512]{0,1:T(8,128)S(1)}, u32[]{:S(2)}, u32[]{:S(2)}) %collective-permute-start.2) | collective-permute-done | bytes 6176 | tf_op jit(solution)/shard_map/ppermute | solution.py:24
  133.3 2.4 divide_multiply_fusion
  137.4 2.7 reshape.145
  141.1 3.4 fusion.36
  144.5 6.9 %while.31 = (s32[]{:T(128)}, f32[4,64,128]{2,1,0:T(8,128)S(1)}, f32[4]{0:T(128)S(1)}, f32[4,4,64,128]{3,2,1,0:T(8,128)}, f32[4,4]{1,0:T(4,128)S(1)}, /*index=5*/...) while((s32[]{:T(128)}, f32[4,64,128]{2,1,0:T(8,128)S(1)}, f32[4]{0:T(128)S(1)}, ...), condition=%wide.region_7.8_spmd.clone, body=%wide.region_6.7_spmd.clone.sunk | while | flops 131083 | bytes 655617 | solution.py:145
  152.7 10.8 %all-reduce.1 = f32[16]{0:T(128)S(1)} all-reduce(f32[16]{0:T(128)S(1)} %dynamic-update-slice), channel_id=2, replica_groups=mesh['seq'=4,'tp'=8] {'seq'}, use_global_device_ids=true, to_apply=%add.1 | all-reduce | flops 16 | bytes 128
  163.6 10.2 %all-gather.1 = f32[16,64,128]{2,1,0:T(8,128)} all-gather(f32[4,64,128]{2,1,0:T(8,128)S(1)} %get-tuple-element.142), channel_id=3, replica_groups=mesh['seq'=4,'tp'=8] {'seq'}, dimensions={0}, use_global_device_ids=true | all-gather | bytes 655360 | tf_op jit(solution)/shard_map/all_gather | solution.py:29
  173.8 3.1 while.32
  178.2 5.2 %fusion.33 = f32[4,256,4,64]{1,3,2,0:T(8,128)S(1)} fusion(f32[4,4,256]{2,1,0:T(4,128)S(1)} %copy.69, f32[4,256,256]{2,1,0:T(8,128)S(1)} %fusion.47, f32[4,4,256]{2,1,0:T(4,128)S(1)} %reduce_window_sum.41, pred[4,256,256]{2,1,0:T(8,128)(4,1)S(1)} %copy-done.11, f32[4,256,4,64]{1,0,3,2:T(4,128)S(1)} %copy-done.8), kind=kOutput, calls=%fused_computation.51 | convolution fusion | flops 810549248 | bytes 3440640 | tf_op jit(solution)/shard_map/chij,cjhp->cihp/dot_general | solution.py:128
  187.3 1.2 collective-permute-done.3
  188.4 8.2 %fusion.46 = f32[1024,4096]{1,0:T(8,128)} fusion(bf16[256,4096]{1,0:T(8,128)(2,1)S(1)} %copy-done, f32[1024,256]{0,1:T(8,128)S(1)} %get-tuple-element.213, f32[256]{0:T(256)S(1)} %copy-done.14, f32[1024]{0:T(1024)S(1)} %add_rsqrt_fusion), kind=kOutput, calls=%fused_computation.67 | convolution fusion | flops 2148270080 | bytes 19928064 | tf_op jit(solution)/shard_map/dot_general | solution.py:162
  196.7 166.2 %reduce-scatter.2.cloned.1.call-done = f32[128,4096]{1,0:T(8,128)} async-done(((f32[1024,4096]{1,0:T(8,128)}), f32[128,4096]{1,0:T(8,128)}) %reduce-scatter.2.cloned.1.call-update) | async-done | bytes 2097168 | tf_op jit(solution)/shard_map/reduce_scatter | solution.py:163
  362.8 2.8 fusion.23
  (135 shorter events, 23.7 us)
Async XLA Ops:
  6.5 181.9 %copy-start = (bf16[256,4096]{1,0:T(8,128)(2,1)S(1)}, bf16[256,4096]{1,0:T(8,128)(2,1)}, u32[]{:S(2)}) copy-start(bf16[256,4096]{1,0:T(8,128)(2,1)} %param.28) | copy-start | bytes 6291460
  6.5 4.3 %copy-start.18 = (bf16[4,128]{1,0:T(4,128)(2,1)S(1)}, bf16[4,128]{1,0:T(4,128)(2,1)}, u32[]{:S(2)}) copy-start(bf16[4,128]{1,0:T(4,128)(2,1)} %param.25) | copy-start | bytes 3076
  6.5 4.9 %copy-start.7 = (bf16[4096,128]{1,0:T(8,128)(2,1)S(1)}, bf16[4096,128]{1,0:T(8,128)(2,1)}, u32[]{:S(2)}) copy-start(bf16[4096,128]{1,0:T(8,128)(2,1)} %param.20) | copy-start | bytes 3145732
  6.5 5.0 %copy-start.12 = (s32[4096]{0:T(1024)S(1)}, s32[4096]{0:T(1024)}, u32[]{:S(2)}) copy-start(s32[4096]{0:T(1024)} %param.29) | copy-start | bytes 49156
  6.5 89.2 %all-gather.4.cloned.1.call-start = ((), (), s32[]{:S(2)}) async-start(), calls=%async_computation.1 | async-start | bytes 9437184 | tf_op jit(solution)/shard_map/all_gather | solution.py:90
  8.3 6.3 %copy-start.19 = (f32[4]{0:T(128)S(1)}, f32[4]{0:T(128)}, u32[]{:S(2)}) copy-start(f32[4]{0:T(128)} %param.26) | copy-start | bytes 52
  10.8 352.0 %reduce-scatter.2.cloned.1.call-start = ((), (), s32[]{:S(2)}) async-start(), calls=%async_computation.2 | async-start | bytes 18874368 | tf_op jit(solution)/shard_map/reduce_scatter | solution.py:163
  10.9 10.1 %collective-permute-start = (bf16[4,128]{1,0:T(4,128)(2,1)S(1)}, bf16[4,128]{1,0:T(4,128)(2,1)S(1)}, u32[]{:S(2)}, u32[]{:S(2)}) collective-permute-start(bf16[4,128]{1,0:T(4,128)(2,1)S(1)} %copy-done.18), channel_id=1, source_target_pairs={{0,1},{1,0},{2,3},{3,2},{4,5},{5,4},{6,7},{7,6},{8,9},{9,8},{10,11... | collective-permute-start | bytes 3080 | tf_op jit(solution)/shard_map/ppermute | solution.py:18
  11.4 95.7 %collective-permute-start.1 = (bf16[4096,128]{1,0:T(8,128)(2,1)S(1)}, bf16[4096,128]{1,0:T(8,128)(2,1)}, u32[]{:S(2)}, u32[]{:S(2)}) collective-permute-start(bf16[4096,128]{1,0:T(8,128)(2,1)S(1)} %copy-done.7), channel_id=1, source_target_pairs={{0,1},{1,0},{2,3},{3,2},{4,5},{5,4},{6,7},{7,6},{8,9},{9,8},{10,11... | collective-permute-start | bytes 3145736 | tf_op jit(solution)/shard_map/ppermute | solution.py:18
  14.8 5.0 %copy-start.20 = (u32[32]{0:T(128)S(1)}, u32[32]{0:T(128)}, u32[]{:S(2)}) copy-start(u32[32]{0:T(128)} %constant.107) | copy-start | bytes 388
  14.8 6.3 %copy-start.17 = (bf16[4,256]{1,0:T(4,128)(2,1)S(1)}, bf16[4,256]{1,0:T(4,128)(2,1)}, u32[]{:S(2)}) copy-start(bf16[4,256]{1,0:T(4,128)(2,1)} %param.24) | copy-start | bytes 6148
  14.8 81.0 %copy-start.13 = (bf16[4096,4]{0,1:T(4,128)(2,1)S(1)}, bf16[4096,4]{0,1:T(4,128)(2,1)}, u32[]{:S(2)}) copy-start(bf16[4096,4]{0,1:T(4,128)(2,1)} %param.21) | copy-start | bytes 98308
  14.8 81.0 %copy-start.15 = (f32[4]{0:T(128)S(1)}, f32[4]{0:T(128)}, u32[]{:S(2)}) copy-start(f32[4]{0:T(128)} %param.23) | copy-start | bytes 52
  14.8 81.0 %copy-start.16 = (f32[4]{0:T(128)S(1)}, f32[4]{0:T(128)}, u32[]{:S(2)}) copy-start(f32[4]{0:T(128)} %param.22) | copy-start | bytes 52
  107.1 6.7 %copy-start.1 = (bf16[1024,4096]{1,0:T(8,128)(2,1)S(1)}, bf16[1024,4096]{1,0:T(8,128)(2,1)}, u32[]{:S(2)}) copy-start(bf16[1024,4096]{1,0:T(8,128)(2,1)} %all-gather.4.cloned.1.call-done) | copy-start | bytes 25165828
  123.3 4.1 %copy-start.4 = (f32[1024,512]{0,1:T(8,128)}, f32[1024,512]{0,1:T(8,128)S(1)}, u32[]{:S(2)}) copy-start(f32[1024,512]{0,1:T(8,128)S(1)} %fusion.78) | copy-start | bytes 6291460
  123.4 9.8 %collective-permute-start.2 = (f32[3,512]{0,1:T(8,128)S(1)}, f32[3,512]{0,1:T(8,128)S(1)}, u32[]{:S(2)}, u32[]{:S(2)}) collective-permute-start(f32[3,512]{0,1:T(8,128)S(1)} %pad_maximum_fusion.3), channel_id=1, source_target_pairs={{0,8},{8,16},{16,24},{1,9},{9,17},{17,25},{2,10},{10,18},{18,26},{... | collective-permute-start | bytes 18440 | tf_op jit(solution)/shard_map/ppermute | solution.py:24
  135.6 1.6 copy-start.2
  178.2 5.2 %copy-start.9 = (f32[4,256,128]{1,0,2:T(4,128)S(1)}, f32[4,256,128]{1,0,2:T(4,128)}, u32[]{:S(2)}) copy-start(f32[4,256,128]{1,0,2:T(4,128)} %reshape.149) | copy-start | bytes 1572868
  178.2 5.2 %copy-start.10 = (f32[4,4,64,128]{3,2,1,0:T(8,128)S(1)}, f32[4,4,64,128]{3,2,1,0:T(8,128)}, u32[]{:S(2)}) copy-start(f32[4,4,64,128]{3,2,1,0:T(8,128)} %get-tuple-element.139) | copy-start | bytes 1572868
  184.6 2.2 copy-start.5
  186.8 1.7 copy-start.14
  187.2 1.2 collective-permute-start.3
  196.7 166.2 %copy-start.6 = (bf16[128,4096]{1,0:T(8,128)(2,1)S(1)}, bf16[128,4096]{1,0:T(8,128)(2,1)}, u32[]{:S(2)}) copy-start(bf16[128,4096]{1,0:T(8,128)(2,1)} %param.17) | copy-start | bytes 3145732
  (3 other events, 4.1 us)
Sparse Core Ops, SparseCore 0:
  10.9 84.7 all-gather.3
  196.8 165.9 reduce-scatter.1
where the time goes:
time: 373 us; the launch traced here: 372 us
  waiting for transfers between devices  248 us (66%)
  matrix products  40.7 us (11%)
  other arithmetic  27.4 us (7%)
  blocking collectives  21.1 us (6%)
  local copies, waits for them, and re-layouts  16.4 us (4%)
  between operations  14.5 us (4%)
  starting transfers between devices  4.37 us (1%)
    reduce_scatter x1, waiting for transfers between devices, body(): mine = lax.psum_scatter(partial_out, 'tp', scatter_dimension=0, tiled=True)  166 us
    all_gather x1, waiting for transfers between devices, body(): piece = lax.all_gather(normed, 'tp', axis=0, tiled=True)  74.7 us
    dot_general x4, matrix products, body(): jnp.dot(piece, matrix, preferred_element_type=jnp.float32)  21.8 us
    unnamed x1, blocking collectives  10.8 us
    all_gather x1, blocking collectives, entering_2(): pieces = jax.tree.map(lambda part: lax.all_gather(part, axis), value)  10.2 us
    unnamed x49, local copies, waits for them, and re-layouts  8.25 us
    dot_general x1, matrix products, body(): jnp.dot(mixed, output_weight, preferred_element_type=jnp.float32)  8.21 us
  transfers between devices with their start and end apart: 6, of which 4 were waited for; matrix products, arithmetic and copies ran while one was open for 5% of the time, Pallas kernels for 0%

commit v1 on v0

--- a/solution.py
+++ b/solution.py
@@ -87,7 +87,21 @@
         axis=1,
     )
     matrices = (inner_weight.reshape(width, 2 * inner_dev),) + group_cols + (step_weight,)
-    piece = lax.all_gather(normed, "tp", axis=0, tiled=True)
+    tall = jax.lax.axis_size("tp")
+    e_now, reply, piece_next = (tall, jax.lax.axis_index("tp"), normed.shape[0])
+    outer, frame_out = (normed, 1)
+    while frame_out < e_now:
+        outer = jnp.concatenate(
+            [
+                outer,
+                jax.lax.ppermute(
+                    outer, "tp", tuple(((d, (d - frame_out) % e_now) for d in range(e_now)))
+                ),
+            ],
+            axis=0,
+        )
+        frame_out = 2 * frame_out
+    piece = jnp.roll(outer, shift=reply * piece_next, axis=0)
     projected = jnp.concatenate(
         [jnp.dot(piece, matrix, preferred_element_type=jnp.float32) for matrix in matrices], axis=1
     )

time: 373 us -> 557 us (1.49)
  waiting for transfers between devices: 248 us -> 398 us
  local copies, waits for them, and re-layouts: 16.4 us -> 34.8 us
  matrix products: 40.7 us -> 48 us
  starting transfers between devices: 4.37 us -> 10 us
    ppermute x0 -> x3, waiting for transfers between devices: none -> 226 us  [body(): jax.lax.ppermute(outer, 'tp', tuple(((d, (d - frame_out) % e_now) for d i...]
    all_gather x1 -> x0, waiting for transfers between devices: 74.7 us -> none  [body(): piece = lax.all_gather(normed, 'tp', axis=0, tiled=True)]
    unnamed x49 -> x55, local copies, waits for them, and re-layouts: 8.25 us -> 22 us
    dot_general x4, matrix products: 21.8 us -> 27.7 us  [body(): jnp.dot(piece, matrix, preferred_element_type=jnp.float32)]
  transfers between devices with their start and end apart: 6 -> 8, of which waited for: 4 -> 6; matrix products, arithmetic and copies ran while one was open for 5% -> 8% of each run, Pallas kernels for 0% -> 0%
where the time goes in v1:
time: 557 us
  waiting for transfers between devices  398 us (71%)
  matrix products  48 us (9%)
  local copies, waits for them, and re-layouts  34.8 us (6%)
  other arithmetic  29.8 us (5%)
  blocking collectives  21.5 us (4%)
  between operations  14.5 us (3%)
  starting transfers between devices  10 us (2%)
    ppermute x3, waiting for transfers between devices, body(): jax.lax.ppermute(outer, 'tp', tuple(((d, (d - frame_out) % e_now) for d i...  226 us
    reduce_scatter x1, waiting for transfers between devices, body(): mine = lax.psum_scatter(partial_out, 'tp', scatter_dimension=0, tiled=True)  166 us
    dot_general x4, matrix products, body(): jnp.dot(piece, matrix, preferred_element_type=jnp.float32)  27.7 us
    unnamed x55, local copies, waits for them, and re-layouts  22 us
    all_gather x1, blocking collectives, entering_2(): pieces = jax.tree.map(lambda part: lax.all_gather(part, axis), value)  12.6 us
  transfers between devices with their start and end apart: 8, of which 6 were waited for; matrix products, arithmetic and copies ran while one was open for 8% of the time, Pallas kernels for 0%

profile of v1, /device:TPU:0, one launch (start us, length us, event | category | flops | bytes accessed | tf_op | source)
XLA Modules:
  0.0 556.6 jit_solution(12788775503215664028)
XLA Ops:
  10.8 4.5 collective-permute-start.1
  15.3 12.3 %collective-permute-done.1 = bf16[128,4096]{1,0:T(8,128)(2,1)S(1)} collective-permute-done((bf16[128,4096]{1,0:T(8,128)(2,1)S(1)}, bf16[128,4096]{1,0:T(8,128)(2,1)S(1)}, u32[]{:S(2)}, u32[]{:S(2)}) %collective-permute-start.1) | collective-permute-done | bytes 1048608 | tf_op jit(solution)/shard_map/ppermute | solution.py:97
  28.5 45.8 %collective-permute-done.2 = bf16[256,4096]{1,0:T(8,128)(2,1)S(1)} collective-permute-done((bf16[256,4096]{1,0:T(8,128)(2,1)S(1)}, bf16[256,4096]{1,0:T(8,128)(2,1)S(1)}, u32[]{:S(2)}, u32[]{:S(2)}) %collective-permute-start.2) | collective-permute-done | bytes 2097184 | tf_op jit(solution)/shard_map/ppermute | solution.py:97
  82.2 4.9 copy.92
  90.9 3.1 constant_dynamic-update-slice_fusion.5
  94.0 167.6 %collective-permute-done.3 = bf16[512,4096]{1,0:T(8,128)(2,1)} collective-permute-done((bf16[512,4096]{1,0:T(8,128)(2,1)}, bf16[512,4096]{1,0:T(8,128)(2,1)}, u32[]{:S(2)}, u32[]{:S(2)}) %collective-permute-start.3) | collective-permute-done | bytes 4194336 | tf_op jit(solution)/shard_map/ppermute | solution.py:97
  261.6 4.7 constant_dynamic-update-slice_fusion.4
  269.9 4.7 constant_dynamic-update-slice_fusion
  274.6 5.7 %negate_multiply_fusion = (f32[1024,4]{0,1:T(4,128)S(1)}, f32[1024,4]{0,1:T(4,128)S(1)}) fusion(f32[4]{0:T(128)S(1)} %copy-done.15, f32[4]{0:T(128)S(1)} %copy-done.16, bf16[4096,4]{0,1:T(4,128)(2,1)S(1)} %copy-done.13, bf16[2048,4096]{1,0:T(8,128)(2,1)} %constant_dynamic-update-slice_fusion, s32[]{:T(128)S(6)} %select_n.93), kind=kOutput, calls=%fused_computation.112 | convolution fusion | flops 33591296 | bytes 8454180 | tf_op jit(solution)/shard_map/dot_general | solution.py:106
  280.3 4.8 reduce-window.14
  285.9 8.3 %fusion.10 = f32[1024,512]{0,1:T(8,128)S(1)} fusion(bf16[4096,512]{1,0:T(8,128)(2,1)} %bitcast.88, bf16[2048,4096]{1,0:T(8,128)(2,1)} %constant_dynamic-update-slice_fusion, s32[]{:T(128)S(6)} %select_n.93), kind=kOutput, calls=%fused_computation.16 | convolution fusion | flops 4294967296 | bytes 14680068 | tf_op jit(solution)/shard_map/dot_general | solution.py:106
  294.2 7.3 %fusion.6 = f32[1024,128]{0,1:T(8,128)S(1)} fusion(bf16[2048,4096]{1,0:T(8,128)(2,1)} %constant_dynamic-update-slice_fusion, s32[]{:T(128)S(6)} %select_n.93, bf16[4096,128]{1,0:T(8,128)(2,1)} %collective-permute-done.4, bf16[4096,128]{1,0:T(8,128)(2,1)} %param.20, pred[]{:T(512)S(6)} %eq.62), kind=kOutput, calls=%fused_computation.12 | convolution fusion | flops 1074266112 | bytes 11010053 | tf_op jit(solution)/shard_map/dot_general | solution.py:106
  301.5 6.5 %fusion.8 = f32[1024,128]{0,1:T(8,128)S(1)} fusion(bf16[2048,4096]{1,0:T(8,128)(2,1)} %constant_dynamic-update-slice_fusion, s32[]{:T(128)S(6)} %select_n.93, bf16[4096,128]{1,0:T(8,128)(2,1)} %param.20, bf16[4096,128]{1,0:T(8,128)(2,1)} %collective-permute-done.4, pred[]{:T(512)S(6)} %eq.62), kind=kOutput, calls=%fused_computation.14 | convolution fusion | flops 1074266112 | bytes 11010053 | tf_op jit(solution)/shard_map/dot_general | solution.py:106
  308.2 3.6 collective-permute-start.5
  312.1 5.2 collective-permute-done.5
  325.2 3.4 fusion.47
  328.5 6.8 %while.31 = (s32[]{:T(128)}, f32[4,64,128]{2,1,0:T(8,128)S(1)}, f32[4]{0:T(128)S(1)}, f32[4,4,64,128]{3,2,1,0:T(8,128)}, f32[4,4]{1,0:T(4,128)S(1)}, /*index=5*/...) while((s32[]{:T(128)}, f32[4,64,128]{2,1,0:T(8,128)S(1)}, f32[4]{0:T(128)S(1)}, ...), condition=%wide.region_7.8_spmd.clone, body=%wide.region_6.7_spmd.clone.sunk | while | flops 131083 | bytes 656117 | solution.py:159
  335.6 12.6 %all-gather.1 = f32[16,64,128]{2,1,0:T(8,128)} all-gather(f32[4,64,128]{2,1,0:T(8,128)S(1)} %get-tuple-element.142), channel_id=3, replica_groups=mesh['seq'=4,'tp'=8] {'seq'}, dimensions={0}, use_global_device_ids=true | all-gather | bytes 655360 | tf_op jit(solution)/shard_map/all_gather | solution.py:29
  348.2 8.9 %all-reduce.1 = f32[16]{0:T(128)S(1)} all-reduce(f32[16]{0:T(128)S(1)} %dynamic-update-slice), channel_id=2, replica_groups=mesh['seq'=4,'tp'=8] {'seq'}, use_global_device_ids=true, to_apply=%add.1 | all-reduce | flops 16 | bytes 128
  357.2 3.1 while.32
  362.3 6.6 %fusion.41 = f32[4,256,4,64]{1,3,2,0:T(8,128)S(1)} fusion(f32[4,4,256]{2,1,0:T(4,128)S(1)} %copy.69, f32[4,256,256]{2,1,0:T(8,128)S(1)} %fusion.56, f32[4,4,256]{2,1,0:T(4,128)S(1)} %reduce_window_sum.41, pred[4,256,256]{2,1,0:T(8,128)(4,1)} %compare_and_fusion, f32[4,256,4,64]{1,0,3,2:T(4,128)} %reshape.145), kind=kOutput, calls=%fused_computation.61 | convolution fusion | flops 810549248 | bytes 3440640 | tf_op jit(solution)/shard_map/chij,cjhp->cihp/dot_general | solution.py:142
  372.8 8.2 %fusion.55 = f32[1024,4096]{1,0:T(8,128)} fusion(bf16[256,4096]{1,0:T(8,128)(2,1)S(1)} %copy-done, f32[1024,256]{0,1:T(8,128)S(1)} %get-tuple-element.213, f32[256]{0:T(256)S(1)} %copy-done.14, f32[1024]{0:T(1024)S(1)} %add_rsqrt_fusion), kind=kOutput, calls=%fused_computation.75 | convolution fusion | flops 2148270080 | bytes 19928064 | tf_op jit(solution)/shard_map/dot_general | solution.py:176
  381.1 165.9 %reduce-scatter.2.cloned.1.call-done = f32[128,4096]{1,0:T(8,128)} async-done(((f32[1024,4096]{1,0:T(8,128)}), f32[128,4096]{1,0:T(8,128)}) %reduce-scatter.2.cloned.1.call-update) | async-done | bytes 2097168 | tf_op jit(solution)/shard_map/reduce_scatter | solution.py:177
  547.0 2.8 fusion.31
  (147 shorter events, 44.8 us)
Async XLA Ops:
  6.5 366.3 %copy-start = (bf16[256,4096]{1,0:T(8,128)(2,1)S(1)}, bf16[256,4096]{1,0:T(8,128)(2,1)}, u32[]{:S(2)}) copy-start(bf16[256,4096]{1,0:T(8,128)(2,1)} %param.28) | copy-start | bytes 6291460
  6.5 540.4 %reduce-scatter.2.cloned.1.call-start = ((), (), s32[]{:S(2)}) async-start(), calls=%async_computation.1 | async-start | bytes 18874368 | tf_op jit(solution)/shard_map/reduce_scatter | solution.py:177
  10.8 16.8 %collective-permute-start.1 = (bf16[128,4096]{1,0:T(8,128)(2,1)S(1)}, bf16[128,4096]{1,0:T(8,128)(2,1)S(1)}, u32[]{:S(2)}, u32[]{:S(2)}) collective-permute-start(bf16[128,4096]{1,0:T(8,128)(2,1)S(1)} %get-tuple-element.218), channel_id=1, source_target_pairs={{0,7},{1,0},{2,1},{3,2},{4,3},{5,4},{6,5},{7,6},{8,15},{9,8},{10,9... | collective-permute-start | bytes 3145736 | tf_op jit(solution)/shard_map/ppermute | solution.py:97
  27.6 50.1 %copy-start.3 = (bf16[128,4096]{1,0:T(8,128)(2,1)}, bf16[128,4096]{1,0:T(8,128)(2,1)S(1)}, u32[]{:S(2)}) copy-start(bf16[128,4096]{1,0:T(8,128)(2,1)S(1)} %collective-permute-done.1) | copy-start | bytes 3145732
  27.8 51.2 %copy-start.18 = (bf16[4,128]{1,0:T(4,128)(2,1)S(1)}, bf16[4,128]{1,0:T(4,128)(2,1)}, u32[]{:S(2)}) copy-start(bf16[4,128]{1,0:T(4,128)(2,1)} %param.25) | copy-start | bytes 3076
  27.8 51.2 %copy-start.12 = (s32[4096]{0:T(1024)S(1)}, s32[4096]{0:T(1024)}, u32[]{:S(2)}) copy-start(s32[4096]{0:T(1024)} %param.29) | copy-start | bytes 49156
  27.9 46.4 %collective-permute-start.2 = (bf16[256,4096]{1,0:T(8,128)(2,1)S(1)}, bf16[256,4096]{1,0:T(8,128)(2,1)S(1)}, u32[]{:S(2)}, u32[]{:S(2)}) collective-permute-start(bf16[256,4096]{1,0:T(8,128)(2,1)S(1)} %pad_maximum_fusion.4), channel_id=1, source_target_pairs={{0,6},{1,7},{2,0},{3,1},{4,2},{5,3},{6,4},{7,5},{8,14},{9,15},{10,... | collective-permute-start | bytes 6291464 | tf_op jit(solution)/shard_map/ppermute | solution.py:97
  77.8 183.8 %collective-permute-start.3 = (bf16[512,4096]{1,0:T(8,128)(2,1)}, bf16[512,4096]{1,0:T(8,128)(2,1)}, u32[]{:S(2)}, u32[]{:S(2)}) collective-permute-start(bf16[512,4096]{1,0:T(8,128)(2,1)} %pad_maximum_fusion), channel_id=1, source_target_pairs={{0,4},{1,5},{2,6},{3,7},{4,0},{5,1},{6,2},{7,3},{8,12},{9,13},{10,... | collective-permute-start | bytes 12582920 | tf_op jit(solution)/shard_map/ppermute | solution.py:97
  77.8 216.4 %collective-permute-start.4 = (bf16[4096,128]{1,0:T(8,128)(2,1)}, bf16[4096,128]{1,0:T(8,128)(2,1)}, u32[]{:S(2)}, u32[]{:S(2)}) collective-permute-start(bf16[4096,128]{1,0:T(8,128)(2,1)} %param.20), channel_id=1, source_target_pairs={{0,1},{1,0},{2,3},{3,2},{4,5},{5,4},{6,7},{7,6},{8,9},{9,8},{10,11... | collective-permute-start | bytes 3145736 | tf_op jit(solution)/shard_map/ppermute | solution.py:18
  79.0 9.5 %collective-permute-start = (bf16[4,128]{1,0:T(4,128)(2,1)S(1)}, bf16[4,128]{1,0:T(4,128)(2,1)S(1)}, u32[]{:S(2)}, u32[]{:S(2)}) collective-permute-start(bf16[4,128]{1,0:T(4,128)(2,1)S(1)} %copy-done.18), channel_id=1, source_target_pairs={{0,1},{1,0},{2,3},{3,2},{4,5},{5,4},{6,7},{7,6},{8,9},{9,8},{10,11... | collective-permute-start | bytes 3080 | tf_op jit(solution)/shard_map/ppermute | solution.py:18
  82.2 4.9 copy-start.19
  82.2 5.1 copy-start.20
  82.2 6.3 %copy-start.17 = (bf16[4,256]{1,0:T(4,128)(2,1)S(1)}, bf16[4,256]{1,0:T(4,128)(2,1)}, u32[]{:S(2)}) copy-start(bf16[4,256]{1,0:T(4,128)(2,1)} %param.24) | copy-start | bytes 6148
  94.0 173.4 %copy-start.4 = (bf16[128,4096]{1,0:T(8,128)(2,1)S(1)}, bf16[128,4096]{1,0:T(8,128)(2,1)}, u32[]{:S(2)}) copy-start(bf16[128,4096]{1,0:T(8,128)(2,1)} %copy-done.3) | copy-start | bytes 3145732
  269.9 4.7 copy-start.13
  269.9 4.7 copy-start.15
  269.9 4.7 copy-start.16
  294.2 17.7 %copy-start.7 = (f32[1024,512]{0,1:T(8,128)}, f32[1024,512]{0,1:T(8,128)S(1)}, u32[]{:S(2)}) copy-start(f32[1024,512]{0,1:T(8,128)S(1)} %fusion.10) | copy-start | bytes 6291460
  308.2 9.2 %collective-permute-start.5 = (f32[3,512]{0,1:T(8,128)S(1)}, f32[3,512]{0,1:T(8,128)S(1)}, u32[]{:S(2)}, u32[]{:S(2)}) collective-permute-start(f32[3,512]{0,1:T(8,128)S(1)} %pad_maximum_fusion.5), channel_id=1, source_target_pairs={{0,8},{8,16},{16,24},{1,9},{9,17},{17,25},{2,10},{10,18},{18,26},{... | collective-permute-start | bytes 18440 | tf_op jit(solution)/shard_map/ppermute | solution.py:24
  362.3 6.6 %copy-start.10 = (f32[4,256,128]{1,0,2:T(4,128)S(1)}, f32[4,256,128]{1,0,2:T(4,128)}, u32[]{:S(2)}) copy-start(f32[4,256,128]{1,0,2:T(4,128)} %reshape.149) | copy-start | bytes 1572868
  362.3 6.6 %copy-start.11 = (f32[4,4,64,128]{3,2,1,0:T(8,128)S(1)}, f32[4,4,64,128]{3,2,1,0:T(8,128)}, u32[]{:S(2)}) copy-start(f32[4,4,64,128]{3,2,1,0:T(8,128)} %get-tuple-element.139) | copy-start | bytes 1572868
  370.1 2.7 copy-start.14
  371.6 1.2 collective-permute-start.6
  381.1 165.9 %copy-start.9 = (bf16[128,4096]{1,0:T(8,128)(2,1)S(1)}, bf16[128,4096]{1,0:T(8,128)(2,1)}, u32[]{:S(2)}) copy-start(bf16[128,4096]{1,0:T(8,128)(2,1)} %param.17) | copy-start | bytes 3145732
  (5 other events, 9.5 us)
Sparse Core Ops, SparseCore 0:
  381.2 165.7 reduce-scatter.1
